TPU v7x, 32 devices: a whole 2x2x4 slice. The times are simulated.
32 devices in a mesh: ens: 2 (over y), grid: 16 (over z, x, core).
Axes of the slice: x: 2, y: 2, z: 4, core: 2. Of those that a mesh axis runs over, the one named last changes fastest.
Arguments:
- fields: bfloat16 [2, 384, 768, 256], P('ens', 'grid'), may hold values from -6 to 6
- mode_counts: int32 [384], P('grid'), may hold values from 96 to 384, as said below
- gain_attn: float32 [256], replicated, may hold values from 0.5 to 1.5
- w_query: bfloat16 [256, 256], replicated, may hold values from -1 to 1
- w_key: bfloat16 [256, 256], replicated, may hold values from -8 to 8
- w_value: bfloat16 [256, 256], replicated, may hold values from -0.375 to 0.375
- w_out: bfloat16 [256, 256], replicated, may hold values from -0.375 to 0.375
- gain_spec: float32 [256], replicated, may hold values from 0.5 to 1.5
- w_first: bfloat16 [2, 8, 32, 32], replicated, may hold values from -1 to 1
- w_second: bfloat16 [2, 8, 32, 32], replicated, may hold values from -1 to 1
Outputs:
- layer_out: bfloat16 [2, 384, 768, 256], P('ens', 'grid')
Inputs may be any that keep to these rules, and one draw needn't show every extreme that they name: `mode_counts`: longitude wavenumbers kept in each latitude row; some row keeps all 384.
All inputs are finite; a program needn't handle non-finite values.
Results may differ from a plain program's by a relative error of at most 0.012.
Values may be sent and summed in bfloat16 or wider, within the bound.
A program may use at most 256 MiB of HBM per device.

v0:
```python
import math
import jax
import jax.numpy as jnp
from jax import lax
from jax.sharding import PartitionSpec as P

HEAD = 32
NLAT = 384
KLON = 384
KLAT = 128
norm_eps = 1e-05


def layer_norm(inputs, gain_vec):
    widened = inputs.astype(jnp.float32)
    center = widened - jnp.mean(widened, axis=-1, keepdims=True)
    spread = jnp.mean(center * center, axis=-1, keepdims=True)
    return center * lax.rsqrt(spread + norm_eps) * gain_vec


def lon_table(points, mode_count):
    positions = jnp.arange(points, dtype=jnp.int32)
    frequency = jnp.arange(mode_count, dtype=jnp.int32)
    turn_count = positions[:, None] * frequency[None, :] % points
    angles = 2.0 * math.pi / points * turn_count.astype(jnp.float32)
    factor = 1.0 / math.sqrt(points)
    return jnp.concatenate([jnp.cos(angles) * factor, -jnp.sin(angles) * factor], axis=1).astype(
        jnp.bfloat16
    )


def lon_inverse(points, mode_count):
    positions = jnp.arange(points, dtype=jnp.int32)
    frequency = jnp.arange(mode_count, dtype=jnp.int32)
    turn_count = frequency[:, None] * positions[None, :] % points
    angles = 2.0 * math.pi / points * turn_count.astype(jnp.float32)
    weight = jnp.where(frequency == 0, 1.0, 2.0).astype(jnp.float32)[:, None] / math.sqrt(points)
    return jnp.stack([jnp.cos(angles) * weight, -jnp.sin(angles) * weight]).astype(jnp.bfloat16)


def lat_angles(row_count, mode_count):
    frequency = jnp.arange(mode_count, dtype=jnp.int32)
    frequency = jnp.where(frequency < mode_count // 2, frequency, frequency - mode_count)
    positions = jnp.arange(row_count, dtype=jnp.int32)
    turn_count = frequency[:, None] * positions[None, :] % row_count
    return 2.0 * math.pi / row_count * turn_count.astype(jnp.float32)


def lat_forward(row_count, mode_count):
    angles = lat_angles(row_count, mode_count)
    factor = 1.0 / math.sqrt(row_count)
    cosine = jnp.cos(angles) * factor
    sine_part = jnp.sin(angles) * factor
    return jnp.stack(
        [jnp.stack([cosine, sine_part], axis=1), jnp.stack([-sine_part, cosine], axis=1)]
    ).astype(jnp.bfloat16)


def lat_inverse(row_count, mode_count):
    angles = jnp.transpose(lat_angles(row_count, mode_count))
    factor = 1.0 / math.sqrt(row_count)
    cosine = jnp.cos(angles) * factor
    sine_part = jnp.sin(angles) * factor
    return jnp.stack([jnp.stack([cosine, -sine_part]), jnp.stack([sine_part, cosine])]).astype(
        jnp.bfloat16
    )


def complex_blocks(weight):
    real_part = weight[0]
    imag_part = weight[1]
    return jnp.stack([jnp.stack([real_part, imag_part]), jnp.stack([-imag_part, real_part])])


def mix_blocks(spec, big):
    blocks = spec.reshape(spec.shape[:4] + (big.shape[2], big.shape[3]))
    out_blocks = jnp.einsum("mpqkbi,psbio->msqkbo", blocks, big, preferred_element_type=jnp.float32)
    return out_blocks.reshape(spec.shape)


def mix_members(all_scores, all_values, head_count):
    members, lat_rows, lon_points, feat_dim = all_values.shape
    row_max = jnp.max(all_scores, axis=0, keepdims=True)
    exps = jnp.exp(all_scores - row_max)
    totals = jnp.sum(exps, axis=0)
    weights = exps.astype(jnp.bfloat16)
    split_values = all_values.reshape(members, lat_rows, lon_points, head_count, HEAD)
    mixed_out = jnp.einsum(
        "nmlhw,nlwhe->mlwhe", weights, split_values, preferred_element_type=jnp.float32
    )
    mixed_out = mixed_out / jnp.transpose(totals, (0, 1, 3, 2))[..., None]
    return mixed_out.astype(jnp.bfloat16).reshape(
        all_scores.shape[1], lat_rows, lon_points, feat_dim
    )


def shards(
    fields, mode_counts, gain_attn, w_query, w_key, w_value, w_out, gain_spec, w_first, w_second
):
    mem_dev, lat_dev, lon_points, feat_dim = fields.shape
    head_count = feat_dim // HEAD
    score_scale = 1.0 / math.sqrt(HEAD)
    normed = layer_norm(fields, gain_attn).astype(jnp.bfloat16)
    queries = jnp.dot(normed, w_query, preferred_element_type=jnp.float32).astype(jnp.bfloat16)
    queries = queries.reshape(mem_dev, lat_dev, lon_points, head_count, HEAD)
    own_keys = jnp.dot(normed, w_key, preferred_element_type=jnp.float32).astype(jnp.bfloat16)
    own_values = jnp.dot(normed, w_value, preferred_element_type=jnp.float32).astype(jnp.bfloat16)
    key_rows = lax.all_gather(own_keys, "ens", axis=0, tiled=True)
    split_keys = key_rows.reshape(key_rows.shape[:3] + (head_count, HEAD))
    scores = (
        jnp.einsum("mlwhe,nlwhe->nmlhw", queries, split_keys, preferred_element_type=jnp.float32)
        * score_scale
    )
    all_values = lax.all_gather(own_values, "ens", axis=0, tiled=True)
    mixed_out = mix_members(scores, all_values, head_count)
    attended = (
        fields.astype(jnp.float32) + jnp.dot(mixed_out, w_out, preferred_element_type=jnp.float32)
    ).astype(jnp.bfloat16)
    retained = (jnp.arange(KLON, dtype=jnp.int32)[None, :] < mode_counts[:, None]).astype(
        jnp.float32
    )
    normed_two = layer_norm(attended, gain_spec).astype(jnp.bfloat16)
    spectrum = jnp.einsum(
        "mlxd,xk->mlkd", normed_two, lon_table(lon_points, KLON), preferred_element_type=jnp.float32
    )
    spectrum = spectrum.reshape(mem_dev, lat_dev, 2, KLON, feat_dim)
    spectrum = (spectrum * retained[None, :, None, :, None]).astype(jnp.bfloat16)
    forward = lat_forward(NLAT, KLAT)
    inverse = lat_inverse(NLAT, KLAT)
    big_one = complex_blocks(w_first)
    big_two = complex_blocks(w_second)
    rows_spec = jnp.einsum(
        "pqrj,mjrkd->mpqkd",
        forward,
        lax.all_to_all(spectrum, "grid", split_axis=3, concat_axis=1, tiled=True),
        preferred_element_type=jnp.float32,
    ).astype(jnp.bfloat16)
    hidden = jnp.maximum(mix_blocks(rows_spec, big_one), 0.0).astype(jnp.bfloat16)
    second = mix_blocks(hidden, big_two).astype(jnp.bfloat16)
    back_rows = jnp.einsum(
        "rpjq,mpqkd->mjrkd", inverse, second, preferred_element_type=jnp.float32
    ).astype(jnp.bfloat16)
    returned = lax.all_to_all(back_rows, "grid", split_axis=1, concat_axis=3, tiled=True)
    returned = returned * retained.astype(jnp.bfloat16)[None, :, None, :, None]
    field_out = jnp.einsum(
        "mjrkd,rkx->mjxd",
        returned,
        lon_inverse(lon_points, KLON),
        preferred_element_type=jnp.float32,
    )
    return (attended.astype(jnp.float32) + field_out).astype(jnp.bfloat16)


def solution(mesh):
    in_specs = (P("ens", "grid", None, None), P("grid"), P(), P(), P(), P(), P(), P(), P(), P())
    out_specs = P("ens", "grid", None, None)
    return jax.shard_map(shards, mesh=mesh, in_specs=in_specs, out_specs=out_specs, check_vma=False)
```

profile of v0, /device:TPU:11, one launch (start us, length us, event | category | flops | bytes accessed | tf_op | source)
XLA Modules:
  0.0 1163.1 jit_solution(6597510635387888419)
XLA Ops:
  6.5 12.6 %copy.142 = bf16[1,24,768,256]{2,3,1,0:T(8,128)(2,1)} copy(bf16[1,24,768,256]{3,2,1,0:T(8,128)(2,1)} %param.10) | data formatting | bytes 18874368 | tf_op args[0]
  19.2 5.2 convert_reduce_fusion.1
  28.2 11.0 convolution_convert_fusion.1
  40.1 13.7 %convolution_convert_fusion.2 = bf16[24,768,256]{2,1,0:T(8,128)(2,1)} fusion(bf16[256,256]{1,0:T(8,128)(2,1)S(1)} %copy-done.11, bf16[1,24,768,256]{2,3,1,0:T(8,128)(2,1)} %copy.142, f32[256]{0:T(256)S(1)} %copy-done.8, f32[24,768]{1,0:T(8,128)S(1)} %add_rsqrt_fusion.1, f32[24,768]{1,0:T(8,128)S(1)} %broadcast_multiply_fusion.1), kind=kOutput, calls=%fused_computation.36 | convolution fusion | flops 2444230656 | bytes 19153920 | tf_op jit(solution)/shard_map/dot_general | solution.py:107
  53.8 5.3 multiply_convert_fusion.1
  59.8 15.2 %bitcast_convert_fusion.3 = f32[24,8,768,32]{2,3,1,0:T(8,128)} fusion(bf16[256,256]{1,0:T(8,128)(2,1)S(1)} %copy-done.4, bf16[1,24,768,256]{2,3,1,0:T(8,128)(2,1)} %copy.142, f32[256]{0:T(256)S(1)} %copy-done.8, f32[24,768]{1,0:T(8,128)S(1)} %add_rsqrt_fusion.1, f32[24,768]{1,0:T(8,128)S(1)} %broadcast_multiply_fusion.1), kind=kOutput, calls=%fused_computation.143 | convolution fusion | flops 2448949248 | bytes 28591104 | tf_op jit(solution)/shard_map/dot_general | solution.py:104
  75.0 189.7 %all-gather.7.cloned.1.call-done = bf16[48,768,256]{2,1,0:T(8,128)(2,1)} async-done(((bf16[24,768,256]{2,1,0:T(8,128)(2,1)}), bf16[48,768,256]{2,1,0:T(8,128)(2,1)}) %all-gather.7.cloned.1.call-update) | async-done | bytes 18874384 | tf_op jit(solution)/shard_map/all_gather | solution.py:108
  264.7 24.2 %copy.207 = bf16[48,768,256]{1,2,0:T(8,128)(2,1)} copy(bf16[48,768,256]{2,1,0:T(8,128)(2,1)} %all-gather.7.cloned.1.call-done) | data formatting | bytes 37748736
  288.9 17.8 %multiply_reduce_fusion.1 = f32[24,8,768,2]{2,1,0,3:T(8,128)S(1)} fusion(bf16[24,8,768,32,2]{2,3,1,0,4:T(8,128)(2,1)} %bitcast.170, f32[24,8,768,32]{2,3,1,0:T(8,128)} %bitcast_convert_fusion.3), kind=kLoop, calls=%fused_computation.1 | loop fusion | flops 28016640 | bytes 38928384
  307.1 183.5 %all-gather.5.cloned.1.call-done = bf16[48,768,256]{2,1,0:T(8,128)(2,1)} async-done(((bf16[24,768,256]{2,1,0:T(8,128)(2,1)}), bf16[48,768,256]{2,1,0:T(8,128)(2,1)}) %all-gather.5.cloned.1.call-update) | async-done | bytes 18874384 | tf_op jit(solution)/shard_map/all_gather | solution.py:114
  490.6 24.6 %copy.206 = bf16[48,768,256]{1,2,0:T(8,128)(2,1)} copy(bf16[48,768,256]{2,1,0:T(8,128)(2,1)} %all-gather.5.cloned.1.call-done) | data formatting | bytes 37748736
  515.2 13.5 %multiply_reduce_fusion = f32[24,768,8,32]{1,3,2,0:T(8,128)S(1)} fusion(bf16[24,768,8,2,32]{1,4,2,0,3:T(8,128)(2,1)} %bitcast.171, f32[24,768,8,2]{1,2,3,0:T(8,128)S(1)} %get-tuple-element.6), kind=kLoop, calls=%fused_computation | loop fusion | flops 23592960 | bytes 38928384 | tf_op jit(solution)/shard_map/nmlhw,nlwhe->mlwhe/dot_general | solution.py:88
  528.8 4.8 divide_convert_fusion
  533.6 20.6 %convert_reduce_fusion = (f32[24,768]{1,0:T(8,128)S(1)}, bf16[1,24,768,256]{2,3,1,0:T(8,128)(2,1)}) fusion(bf16[24,768,256]{1,2,0:T(8,128)(2,1)} %bitcast.172, bf16[256,256]{1,0:T(8,128)(2,1)S(1)} %copy-done, bf16[1,24,768,256]{2,3,1,0:T(8,128)(2,1)} %copy.142), kind=kOutput, calls=%fused_computation.4 | convolution fusion | flops 2439493632 | bytes 28516352 | tf_op jit(solution)/shard_map/dot_general | solution.py:117
  554.2 6.4 fusion.4
  560.6 10.8 fusion.15
  571.4 7.6 multiply_convert_fusion
  579.0 39.1 %copy.160 = bf16[1,24,2,384,256]{4,2,1,0,3:T(2,128)(2,1)} copy(bf16[1,24,2,384,256]{4,3,2,1,0:T(8,128)(2,1)S(1)} %multiply_convert_fusion) | data formatting | bytes 18874368 | tf_op jit(solution)/shard_map/convert_element_type | solution.py:127
  618.1 6.6 all-to-all-start
  627.0 202.5 %all-to-all-done = bf16[1,24,2,384,256]{4,2,1,0,3:T(2,128)(2,1)} async-done(((bf16[1,24,2,384,256]{4,2,1,0,3:T(2,128)(2,1)}), bf16[1,24,2,384,256]{4,2,1,0,3:T(2,128)(2,1)}, u32[]{:S(2)}, u32[]{:S(2)}) %all-to-all-start) | async-done | bytes 9437216 | tf_op jit(solution)/shard_map/all_to_all | solution.py:135
  829.6 10.7 copy.161
  840.3 8.3 copy.162
  848.6 19.5 %bitcast_convert_fusion.2 = bf16[24,256,2,128]{3,1,2,0:T(8,128)(2,1)S(1)} fusion(bf16[384,2,24,256,1]{3,2,1,0,4:T(8,128)(2,1)} %bitcast.178, bf16[1,128,2,384]{3,1,2,0:T(8,128)(2,1)S(1)} %get-tuple-element.14, bf16[1,128,2,384]{3,1,2,0:T(8,128)(2,1)S(1)} %get-tuple-element.13), kind=kOutput, calls=%fused_computation.40 | convolution fusion | flops 2418278400 | bytes 12976128 | tf_op jit(solution)/shard_map/pqrj,mjrkd->mpqkd/dot_general | solution.py:132
  871.1 5.3 fusion.12
  876.4 24.0 %copy.168 = bf16[1,384,2,24,256]{4,2,3,0,1:T(2,128)(2,1)} copy(bf16[1,384,2,24,256]{1,4,2,3,0:T(8,128)(2,1)} %fusion.12) | data formatting | bytes 18874368 | tf_op jit(solution)/shard_map/convert_element_type | solution.py:142
  900.3 5.2 all-to-all-start.1
  905.5 5.1 multiply_convert_fusion.4
  910.6 199.5 %all-to-all-done.1 = bf16[1,384,2,24,256]{4,2,3,0,1:T(2,128)(2,1)} async-done(((bf16[1,384,2,24,256]{4,2,3,0,1:T(2,128)(2,1)}), bf16[1,384,2,24,256]{4,2,3,0,1:T(2,128)(2,1)}, u32[]{:S(2)}, u32[]{:S(2)}) %all-to-all-start.1) | async-done | bytes 9437216 | tf_op jit(solution)/shard_map/all_to_all | solution.py:143
  1110.2 8.9 copy.169
  1119.1 8.6 copy.170
  1127.7 15.6 %fusion.11 = bf16[1,24,768,256]{2,3,1,0:T(8,128)(2,1)} fusion(bf16[1,24,768,256]{2,3,1,0:T(8,128)(2,1)} %get-tuple-element.26, bf16[24,2,384,256]{3,2,1,0:T(8,128)(2,1)} %bitcast.177, bf16[24,384]{1,0:T(8,128)(2,1)S(1)} %copy-done.7, bf16[1,384,768]{1,2,0:T(8,128)(2,1)S(1)} %get-tuple-element.16, bf16[1,384,768]{1,2,0:T(8,128)(2,1)S(1)} %get-tuple-element.15), kind=kOutput, calls=%fused_computation.19 | convolution fusion | flops 7283146752 | bytes 29509632 | tf_op jit(solution)/shard_map/mjrkd,rkx->mjxd/dot_general | solution.py:145
  1143.3 12.6 %copy.172 = bf16[1,24,768,256]{3,2,1,0:T(8,128)(2,1)} copy(bf16[1,24,768,256]{2,3,1,0:T(8,128)(2,1)} %fusion.11) | data formatting | bytes 18874368 | tf_op jit(solution)/shard_map/convert_element_type | solution.py:151
  (53 shorter events, 11.0 us)
Async XLA Ops:
  6.5 527.0 %copy-start = (bf16[256,256]{1,0:T(8,128)(2,1)S(1)}, bf16[256,256]{1,0:T(8,128)(2,1)}, u32[]{:S(2)}) copy-start(bf16[256,256]{1,0:T(8,128)(2,1)} %param.16) | copy-start | bytes 393220
  6.5 258.1 %all-gather.7.cloned.1.call-start = ((), (), s32[]{:S(2)}) async-start(), calls=%async_computation.3 | async-start | bytes 28311552 | tf_op jit(solution)/shard_map/all_gather | solution.py:108
  19.2 6.4 copy-start.2
  19.2 9.0 copy-start.8
  19.2 9.0 copy-start.10
  39.2 0.9 copy-start.11
  39.2 451.4 %all-gather.5.cloned.1.call-start = ((), (), s32[]{:S(2)}) async-start(), calls=%async_computation.2 | async-start | bytes 28311552 | tf_op jit(solution)/shard_map/all_gather | solution.py:114
  53.8 5.3 copy-start.9
  53.8 6.0 copy-start.4
  554.2 6.5 copy-start.3
  554.2 6.5 copy-start.12
  618.1 6.6 copy-start.5
  618.1 6.8 copy-start.6
  618.1 211.5 %all-to-all-start = ((bf16[1,24,2,384,256]{4,2,1,0,3:T(2,128)(2,1)}), bf16[1,24,2,384,256]{4,2,1,0,3:T(2,128)(2,1)}, u32[]{:S(2)}, u32[]{:S(2)}) async-start(bf16[1,24,2,384,256]{4,2,1,0,3:T(2,128)(2,1)} %copy.160), calls=%async_computation | async-start | bytes 18874368 | tf_op jit(solution)/shard_map/all_to_all | solution.py:135
  900.3 209.9 %all-to-all-start.1 = ((bf16[1,384,2,24,256]{4,2,3,0,1:T(2,128)(2,1)}), bf16[1,384,2,24,256]{4,2,3,0,1:T(2,128)(2,1)}, u32[]{:S(2)}, u32[]{:S(2)}) async-start(bf16[1,384,2,24,256]{4,2,3,0,1:T(2,128)(2,1)} %copy.168), calls=%async_computation.1 | async-start | bytes 18874368 | tf_op jit(solution)/shard_map/all_to_all | solution.py:143
  1119.1 8.6 copy-start.7
  1127.7 28.1 %copy-start.1 = (bf16[256,256]{1,0:T(8,128)(2,1)S(1)}, bf16[256,256]{1,0:T(8,128)(2,1)}, u32[]{:S(2)}) copy-start(bf16[256,256]{1,0:T(8,128)(2,1)} %param.16) | copy-start | bytes 393220
Sparse Core Ops, SparseCore 0:
  39.3 225.2 all-gather.6
  266.2 224.3 all-gather.4
where the time goes:
time: 1170 us; the launch traced here: 1160 us
  waiting for transfers between devices  775 us (66%)
  local copies, waits for them, and re-layouts  177 us (15%)
  matrix products  114 us (10%)
  other arithmetic  71.3 us (6%)
  between operations  14.1 us (1%)
  starting transfers between devices  11.8 us (1%)
    all_to_all x1, waiting for transfers between devices, shards(): lax.all_to_all(spectrum, 'grid', split_axis=3, concat_axis=1, tiled=True)  203 us
    all_to_all x1, waiting for transfers between devices, shards(): lax.all_to_all(back_rows, 'grid', split_axis=1, concat_axis=3, tiled=True)  200 us
    all_gather x1, waiting for transfers between devices, shards(): key_rows = lax.all_gather(own_keys, 'ens', axis=0, tiled=True)  190 us
    all_gather x1, waiting for transfers between devices, shards(): all_values = lax.all_gather(own_values, 'ens', axis=0, tiled=True)  184 us
    unnamed x31, local copies, waits for them, and re-layouts  63.8 us
    convert_element_type x1, local copies, waits for them, and re-layouts, shards(): (spectrum * retained[None, :, None, :, None]).astype(jnp.bfloat16)  39.1 us
    convert_element_type x1, local copies, waits for them, and re-layouts, shards(): back_rows = jnp.einsum('rpjq,mpqkd->mjrkd', inverse, second, preferred_el...  24 us
  transfers between devices with their start and end apart: 4, of which 4 were waited for; matrix products, arithmetic and copies ran while one was open for 7% of the time, Pallas kernels for 0%

commit v1 on v0

--- a/solution.py
+++ b/solution.py
@@ -140,7 +140,12 @@
     back_rows = jnp.einsum(
         "rpjq,mpqkd->mjrkd", inverse, second, preferred_element_type=jnp.float32
     ).astype(jnp.bfloat16)
-    returned = lax.all_to_all(back_rows, "grid", split_axis=1, concat_axis=3, tiled=True)
+    returned = jnp.concatenate(
+        lax.all_to_all(
+            jnp.stack(jnp.split(back_rows, lax.axis_size("grid"), axis=1)), "grid", 0, 0
+        ),
+        axis=3,
+    )
     returned = returned * retained.astype(jnp.bfloat16)[None, :, None, :, None]
     field_out = jnp.einsum(
         "mjrkd,rkx->mjxd",

time: 1170 us -> 1250 us (1.068)
  local copies, waits for them, and re-layouts: 177 us -> 267 us
    another operation x0 -> x18, local copies, waits for them, and re-layouts: none -> 100 us  [shards(): jnp.stack(jnp.split(back_rows, lax.axis_size('grid'), axis=1))]
    convert_element_type x1 -> x0, local copies, waits for them, and re-layouts: 24 us -> none  [shards(): back_rows = jnp.einsum('rpjq,mpqkd->mjrkd', inverse, second, preferred_el...]
    unnamed x31 -> x62, local copies, waits for them, and re-layouts: 63.8 us -> 86.5 us
where the time goes in v1:
time: 1250 us; the launch traced here: 1240 us
  waiting for transfers between devices  774 us (62%)
  local copies, waits for them, and re-layouts  267 us (21%)
  matrix products  104 us (8%)
  other arithmetic  71.1 us (6%)
  between operations  14 us (1%)
    all_to_all x1, waiting for transfers between devices, shards(): lax.all_to_all(spectrum, 'grid', split_axis=3, concat_axis=1, tiled=True)  203 us
    all_to_all x1, waiting for transfers between devices, shards(): lax.all_to_all(jnp.stack(jnp.split(back_rows, lax.axis_size('grid'), axis...  200 us
    all_gather x1, waiting for transfers between devices, shards(): key_rows = lax.all_gather(own_keys, 'ens', axis=0, tiled=True)  190 us
    all_gather x1, waiting for transfers between devices, shards(): all_values = lax.all_gather(own_values, 'ens', axis=0, tiled=True)  182 us
    another operation x18, local copies, waits for them, and re-layouts, shards(): jnp.stack(jnp.split(back_rows, lax.axis_size('grid'), axis=1))  100 us
    unnamed x62, local copies, waits for them, and re-layouts  86.5 us
    convert_element_type x1, local copies, waits for them, and re-layouts, shards(): (spectrum * retained[None, :, None, :, None]).astype(jnp.bfloat16)  39.1 us
  transfers between devices with their start and end apart: 4, of which 4 were waited for; matrix products, arithmetic and copies ran while one was open for 7% of the time, Pallas kernels for 0%

profile of v1, /device:TPU:11, one launch (start us, length us, event | category | flops | bytes accessed | tf_op | source)
XLA Modules:
  0.0 1241.9 jit_solution(271179578393088333)
XLA Ops:
  6.5 12.6 %copy.212 = bf16[1,24,768,256]{2,3,1,0:T(8,128)(2,1)} copy(bf16[1,24,768,256]{3,2,1,0:T(8,128)(2,1)} %param.10) | data formatting | bytes 18874368 | tf_op args[0]
  19.2 5.2 convert_reduce_fusion.1
  28.2 11.0 convolution_convert_fusion.1
  40.1 13.7 %convolution_convert_fusion.2 = bf16[24,768,256]{2,1,0:T(8,128)(2,1)} fusion(bf16[256,256]{1,0:T(8,128)(2,1)S(1)} %copy-done.19, bf16[1,24,768,256]{2,3,1,0:T(8,128)(2,1)} %copy.212, f32[256]{0:T(256)S(1)} %copy-done.16, f32[24,768]{1,0:T(8,128)S(1)} %add_rsqrt_fusion.1, f32[24,768]{1,0:T(8,128)S(1)} %broadcast_multiply_fusion.1), kind=kOutput, calls=%fused_computation.36 | convolution fusion | flops 2444230656 | bytes 19153920 | tf_op jit(solution)/shard_map/dot_general | solution.py:107
  53.8 5.2 multiply_convert_fusion.1
  59.7 15.2 %bitcast_convert_fusion.3 = f32[24,8,768,32]{2,3,1,0:T(8,128)} fusion(bf16[256,256]{1,0:T(8,128)(2,1)S(1)} %copy-done.12, bf16[1,24,768,256]{2,3,1,0:T(8,128)(2,1)} %copy.212, f32[256]{0:T(256)S(1)} %copy-done.16, f32[24,768]{1,0:T(8,128)S(1)} %add_rsqrt_fusion.1, f32[24,768]{1,0:T(8,128)S(1)} %broadcast_multiply_fusion.1), kind=kOutput, calls=%fused_computation.175 | convolution fusion | flops 2448949248 | bytes 28591104 | tf_op jit(solution)/shard_map/dot_general | solution.py:104
  74.9 189.7 %all-gather.7.cloned.1.call-done = bf16[48,768,256]{2,1,0:T(8,128)(2,1)} async-done(((bf16[24,768,256]{2,1,0:T(8,128)(2,1)}), bf16[48,768,256]{2,1,0:T(8,128)(2,1)}) %all-gather.7.cloned.1.call-update) | async-done | bytes 18874384 | tf_op jit(solution)/shard_map/all_gather | solution.py:108
  264.7 25.7 %copy.291 = bf16[48,768,256]{1,2,0:T(8,128)(2,1)} copy(bf16[48,768,256]{2,1,0:T(8,128)(2,1)} %all-gather.7.cloned.1.call-done) | data formatting | bytes 37748736
  290.3 17.7 %multiply_reduce_fusion.1 = f32[24,8,768,2]{2,1,0,3:T(8,128)S(1)} fusion(bf16[24,8,768,32,2]{2,3,1,0,4:T(8,128)(2,1)} %bitcast.201, f32[24,8,768,32]{2,3,1,0:T(8,128)} %bitcast_convert_fusion.3), kind=kLoop, calls=%fused_computation.1 | loop fusion | flops 28016640 | bytes 38928384
  308.4 182.2 %all-gather.5.cloned.1.call-done = bf16[48,768,256]{2,1,0:T(8,128)(2,1)} async-done(((bf16[24,768,256]{2,1,0:T(8,128)(2,1)}), bf16[48,768,256]{2,1,0:T(8,128)(2,1)}) %all-gather.5.cloned.1.call-update) | async-done | bytes 18874384 | tf_op jit(solution)/shard_map/all_gather | solution.py:114
  490.6 24.2 %copy.290 = bf16[48,768,256]{1,2,0:T(8,128)(2,1)} copy(bf16[48,768,256]{2,1,0:T(8,128)(2,1)} %all-gather.5.cloned.1.call-done) | data formatting | bytes 37748736
  514.8 13.5 %multiply_reduce_fusion = f32[24,768,8,32]{1,3,2,0:T(8,128)S(1)} fusion(bf16[24,768,8,2,32]{1,4,2,0,3:T(8,128)(2,1)} %bitcast.202, f32[24,768,8,2]{1,2,3,0:T(8,128)S(1)} %get-tuple-element.22), kind=kLoop, calls=%fused_computation | loop fusion | flops 23592960 | bytes 38928384 | tf_op jit(solution)/shard_map/nmlhw,nlwhe->mlwhe/dot_general | solution.py:88
  528.4 4.8 divide_convert_fusion
  533.2 11.1 convert_reduce_fusion
  544.3 6.4 fusion.4
  550.7 10.8 fusion.15
  561.5 7.6 multiply_convert_fusion
  569.1 39.1 %copy.230 = bf16[1,24,2,384,256]{4,2,1,0,3:T(2,128)(2,1)} copy(bf16[1,24,2,384,256]{4,3,2,1,0:T(8,128)(2,1)S(1)} %multiply_convert_fusion) | data formatting | bytes 18874368 | tf_op jit(solution)/shard_map/convert_element_type | solution.py:127
  608.2 6.6 all-to-all-start
  617.1 202.5 %all-to-all-done = bf16[1,24,2,384,256]{4,2,1,0,3:T(2,128)(2,1)} async-done(((bf16[1,24,2,384,256]{4,2,1,0,3:T(2,128)(2,1)}), bf16[1,24,2,384,256]{4,2,1,0,3:T(2,128)(2,1)}, u32[]{:S(2)}, u32[]{:S(2)}) %all-to-all-start) | async-done | bytes 9437216 | tf_op jit(solution)/shard_map/all_to_all | solution.py:135
  819.7 10.8 copy.231
  830.4 8.3 copy.232
  838.7 19.7 %bitcast_convert_fusion.2 = bf16[24,256,2,128]{3,1,2,0:T(8,128)(2,1)S(1)} fusion(bf16[384,2,24,256,1]{3,2,1,0,4:T(8,128)(2,1)} %bitcast.208, bf16[1,128,2,384]{3,1,2,0:T(8,128)(2,1)S(1)} %get-tuple-element.30, bf16[1,128,2,384]{3,1,2,0:T(8,128)(2,1)S(1)} %get-tuple-element.29), kind=kOutput, calls=%fused_computation.40 | convolution fusion | flops 2418278400 | bytes 12976128 | tf_op jit(solution)/shard_map/pqrj,mjrkd->mpqkd/dot_general | solution.py:132
  861.5 5.1 fusion.12
  866.6 35.9 %slice_bitcast_fusion = (bf16[1,1,24,2,24,256]{2,5,3,4,1,0:T(8,128)(2,1)}, bf16[1,1,24,2,24,256]{2,5,3,4,1,0:T(8,128)(2,1)}, bf16[1,1,24,2,24,256]{2,5,3,4,1,0:T...) fusion(bf16[1,384,2,24,256]{1,4,2,3,0:T(8,128)(2,1)} %fusion.12), kind=kLoop, calls=%fused_computation.44 | loop fusion | bytes 18874368 | tf_op jit(solution)/shard_map/stack | solution.py:145
  902.5 4.1 copy.253
  988.3 5.1 all-to-all-start.1
  993.4 5.1 multiply_convert_fusion.4
  998.6 199.5 %all-to-all-done.1 = bf16[16,1,24,2,24,256]{5,4,3,2,1,0:T(8,128)(2,1)} async-done(((bf16[16,1,24,2,24,256]{5,4,3,2,1,0:T(8,128)(2,1)}), bf16[16,1,24,2,24,256]{5,4,3,2,1,0:T(8,128)(2,1)}, u32[]{:S(2)}, u32[]{:S(2)}) %all-to-all-start.1) | async-done | bytes 9437216 | tf_op jit(solution)/shard_map/all_to_all | solution.py:144
  1198.1 8.6 copy.254
  1206.7 15.6 %fusion.11 = bf16[1,24,768,256]{2,3,1,0:T(8,128)(2,1)} fusion(bf16[1,24,768,256]{2,3,1,0:T(8,128)(2,1)} %get-tuple-element.42, bf16[24,2,384,256]{3,2,1,0:T(8,128)(2,1)} %bitcast.207, bf16[24,384]{1,0:T(8,128)(2,1)S(1)} %copy-done.15, bf16[1,384,768]{1,2,0:T(8,128)(2,1)S(1)} %get-tuple-element.32, bf16[1,384,768]{1,2,0:T(8,128)(2,1)S(1)} %get-tuple-element.31), kind=kOutput, calls=%fused_computation.19 | convolution fusion | flops 7283146752 | bytes 29509632 | tf_op jit(solution)/shard_map/mjrkd,rkx->mjxd/dot_general | solution.py:150
  1222.2 12.6 %copy.256 = bf16[1,24,768,256]{3,2,1,0:T(8,128)(2,1)} copy(bf16[1,24,768,256]{2,3,1,0:T(8,128)(2,1)} %fusion.11) | data formatting | bytes 18874368 | tf_op jit(solution)/shard_map/convert_element_type | solution.py:156
  (100 shorter events, 92.7 us)
Async XLA Ops:
  6.5 526.6 %copy-start = (bf16[256,256]{1,0:T(8,128)(2,1)S(1)}, bf16[256,256]{1,0:T(8,128)(2,1)}, u32[]{:S(2)}) copy-start(bf16[256,256]{1,0:T(8,128)(2,1)} %param.16) | copy-start | bytes 393220
  6.5 258.1 %all-gather.7.cloned.1.call-start = ((), (), s32[]{:S(2)}) async-start(), calls=%async_computation.3 | async-start | bytes 28311552 | tf_op jit(solution)/shard_map/all_gather | solution.py:108
  19.2 6.4 copy-start.2
  19.2 9.0 copy-start.16
  19.2 9.0 copy-start.18
  39.2 0.9 copy-start.19
  39.2 451.4 %all-gather.5.cloned.1.call-start = ((), (), s32[]{:S(2)}) async-start(), calls=%async_computation.2 | async-start | bytes 28311552 | tf_op jit(solution)/shard_map/all_gather | solution.py:114
  53.8 5.2 copy-start.17
  53.8 5.9 copy-start.12
  544.2 6.5 copy-start.3
  544.2 6.5 copy-start.20
  608.2 6.6 copy-start.13
  608.2 6.8 copy-start.14
  608.2 211.5 %all-to-all-start = ((bf16[1,24,2,384,256]{4,2,1,0,3:T(2,128)(2,1)}), bf16[1,24,2,384,256]{4,2,1,0,3:T(2,128)(2,1)}, u32[]{:S(2)}, u32[]{:S(2)}) async-start(bf16[1,24,2,384,256]{4,2,1,0,3:T(2,128)(2,1)} %copy.230), calls=%async_computation | async-start | bytes 18874368 | tf_op jit(solution)/shard_map/all_to_all | solution.py:135
  965.7 15.6 %copy-start.11 = (bf16[1,1,24,2,24,256]{5,4,3,2,1,0:T(8,128)(2,1)S(1)}, bf16[1,1,24,2,24,256]{5,4,3,2,1,0:T(8,128)(2,1)}, u32[]{:S(2)}) copy-start(bf16[1,1,24,2,24,256]{5,4,3,2,1,0:T(8,128)(2,1)} %copy.246) | copy-start | bytes 1769476
  965.7 16.5 %copy-start.10 = (bf16[1,1,24,2,24,256]{5,4,3,2,1,0:T(8,128)(2,1)S(1)}, bf16[1,1,24,2,24,256]{5,4,3,2,1,0:T(8,128)(2,1)}, u32[]{:S(2)}) copy-start(bf16[1,1,24,2,24,256]{5,4,3,2,1,0:T(8,128)(2,1)} %copy.247) | copy-start | bytes 1769476
  965.7 17.3 %copy-start.9 = (bf16[1,1,24,2,24,256]{5,4,3,2,1,0:T(8,128)(2,1)S(1)}, bf16[1,1,24,2,24,256]{5,4,3,2,1,0:T(8,128)(2,1)}, u32[]{:S(2)}) copy-start(bf16[1,1,24,2,24,256]{5,4,3,2,1,0:T(8,128)(2,1)} %copy.248) | copy-start | bytes 1769476
  965.7 18.2 %copy-start.8 = (bf16[1,1,24,2,24,256]{5,4,3,2,1,0:T(8,128)(2,1)S(1)}, bf16[1,1,24,2,24,256]{5,4,3,2,1,0:T(8,128)(2,1)}, u32[]{:S(2)}) copy-start(bf16[1,1,24,2,24,256]{5,4,3,2,1,0:T(8,128)(2,1)} %copy.249) | copy-start | bytes 1769476
  965.7 19.1 %copy-start.7 = (bf16[1,1,24,2,24,256]{5,4,3,2,1,0:T(8,128)(2,1)S(1)}, bf16[1,1,24,2,24,256]{5,4,3,2,1,0:T(8,128)(2,1)}, u32[]{:S(2)}) copy-start(bf16[1,1,24,2,24,256]{5,4,3,2,1,0:T(8,128)(2,1)} %copy.250) | copy-start | bytes 1769476
  965.7 19.9 %copy-start.6 = (bf16[1,1,24,2,24,256]{5,4,3,2,1,0:T(8,128)(2,1)S(1)}, bf16[1,1,24,2,24,256]{5,4,3,2,1,0:T(8,128)(2,1)}, u32[]{:S(2)}) copy-start(bf16[1,1,24,2,24,256]{5,4,3,2,1,0:T(8,128)(2,1)} %copy.251) | copy-start | bytes 1769476
  965.7 20.8 %copy-start.5 = (bf16[1,1,24,2,24,256]{5,4,3,2,1,0:T(8,128)(2,1)S(1)}, bf16[1,1,24,2,24,256]{5,4,3,2,1,0:T(8,128)(2,1)}, u32[]{:S(2)}) copy-start(bf16[1,1,24,2,24,256]{5,4,3,2,1,0:T(8,128)(2,1)} %copy.252) | copy-start | bytes 1769476
  965.7 21.7 %copy-start.4 = (bf16[1,1,24,2,24,256]{5,4,3,2,1,0:T(8,128)(2,1)S(1)}, bf16[1,1,24,2,24,256]{5,4,3,2,1,0:T(8,128)(2,1)}, u32[]{:S(2)}) copy-start(bf16[1,1,24,2,24,256]{5,4,3,2,1,0:T(8,128)(2,1)} %copy.253) | copy-start | bytes 1769476
  988.3 209.8 %all-to-all-start.1 = ((bf16[16,1,24,2,24,256]{5,4,3,2,1,0:T(8,128)(2,1)}), bf16[16,1,24,2,24,256]{5,4,3,2,1,0:T(8,128)(2,1)}, u32[]{:S(2)}, u32[]{:S(2)}) async-start(bf16[16,1,24,2,24,256]{5,4,3,2,1,0:T(8,128)(2,1)} %constant_dynamic-update-slice_fusion), calls=%async_computation.1 | async-start | bytes 18874368 | tf_op jit(solution)/shard_map/all_to_all | solution.py:144
  998.5 208.1 %copy-start.15 = (bf16[24,384]{1,0:T(8,128)(2,1)S(1)}, bf16[24,384]{1,0:T(8,128)(2,1)}, u32[]{:S(2)}) copy-start(bf16[24,384]{1,0:T(8,128)(2,1)} %get-tuple-element.33) | copy-start | bytes 55300
  1206.7 28.2 %copy-start.1 = (bf16[256,256]{1,0:T(8,128)(2,1)S(1)}, bf16[256,256]{1,0:T(8,128)(2,1)}, u32[]{:S(2)}) copy-start(bf16[256,256]{1,0:T(8,128)(2,1)} %param.16) | copy-start | bytes 393220
Sparse Core Ops, SparseCore 0:
  39.3 225.2 all-gather.6
  266.2 224.3 all-gather.4
